TPU v7x, 32 devices: a whole 2x2x4 slice. The times are simulated.
32 devices in a mesh: sector: 8 (over y, x, core), term: 4 (over z).
Axes of the slice: x: 2, y: 2, z: 4, core: 2. Of those that a mesh axis runs over, the one named last changes fastest.
Arguments:
- wave: float32 [8, 512, 512], P('sector', 'term'), may hold values from -12 to 12
- left_ops: bfloat16 [16, 8, 512, 512], P('term', 'sector'), may hold values from -4 to 4
- right_ops: bfloat16 [16, 8, 512, 512], P('term', 'sector'), may hold values from -4 to 4
- charges: int32 [16], replicated, may hold values from -1 to 1, as said below
- diag: float32 [8, 512, 512], P('sector', 'term'), may hold values from 0.5 to 8
Outputs:
- psi_out: float32 [8, 512, 512], P('sector', 'term')
Inputs may be any that keep to these rules, and one draw needn't show every extreme that they name: `charges`: exactly (17) // 2 terms have charge 0; at least one term has charge 1 and at least one has charge -1.
All inputs are finite; a program needn't handle non-finite values.
Results may differ from a plain program's by a relative error of at most 0.0085.
Values may be sent and summed in bfloat16 or wider, within the bound.
No kernel may reach another device: no remote copies, remote signals or barrier semaphores. Data moves between devices by JAX's collectives and lax.ppermute only.
A program may use at most 64 MiB of HBM per device.

v0:
```python
import jax
import jax.numpy as jnp
from jax import lax
from jax.sharding import PartitionSpec as P

STEPS = 3


def from_behind(value, axis, steps):
    count = lax.axis_size(axis)
    leading, last = (max(0, -steps), min(count, count - steps))
    return lax.ppermute(value, axis, [(source, source + steps) for source in range(leading, last)])


def apply_terms(left_ops, right_ops, my_charges, own, lower, upper):
    stacked = jnp.stack([upper, own, lower])
    picked = stacked[my_charges + 1]
    inner = jnp.einsum(
        "tij,tjk->tik", left_ops[:, 0], picked, preferred_element_type=jnp.float32
    ).astype(jnp.bfloat16)
    image = jnp.einsum("tij,tkj->tik", inner, right_ops[:, 0], preferred_element_type=jnp.float32)
    return jnp.sum(image, axis=0)


def per_device(wave, left_ops, right_ops, charges, diag):
    per_dev = left_ops.shape[0]
    my_charges = lax.dynamic_slice_in_dim(charges, lax.axis_index("term") * per_dev, per_dev)
    psi, full_diag = (
        lax.all_gather(wave[0], "term", axis=0, tiled=True),
        lax.all_gather(diag[0], "term", axis=0, tiled=True),
    )
    for step in range(STEPS):
        wb = psi.astype(jnp.bfloat16)
        lower = from_behind(wb, "sector", 1)
        upper = from_behind(wb, "sector", -1)
        partial_image = apply_terms(left_ops, right_ops, my_charges, wb, lower, upper)
        hpsi = lax.psum(partial_image, "term")
        cross, square = lax.psum((jnp.sum(psi * hpsi), jnp.sum(psi * psi)), "sector")
        theta = cross / square
        fresh = psi - (hpsi - theta * psi) / jnp.maximum(jnp.abs(full_diag - theta), 1.0)
        total = lax.psum(jnp.sum(fresh * fresh), "sector")
        psi = fresh / jnp.sqrt(total / (lax.axis_size("sector") * fresh.size) + 1e-06)
    rows_dev = wave.shape[1]
    result = lax.dynamic_slice_in_dim(psi, lax.axis_index("term") * rows_dev, rows_dev, 0)
    return result[None]


def solution(mesh):
    in_specs = (
        P("sector", "term", None),
        P("term", "sector", None, None),
        P("term", "sector", None, None),
        P(),
        P("sector", "term", None),
    )
    out_specs = P("sector", "term", None)
    return jax.shard_map(
        per_device, mesh=mesh, in_specs=in_specs, out_specs=out_specs, check_vma=False
    )
```

profile of v0, /device:TPU:0, one launch (start us, length us, event | category | flops | bytes accessed | tf_op | source)
XLA Modules:
  0.0 397.1 jit_solution(17423861717904664301)
XLA Ops:
  7.3 32.3 %all-gather.5.cloned.1.call-done = f32[1,512,512]{2,1,0:T(8,128)} async-done(((f32[1,128,512]{2,1,0:T(8,128)}), f32[1,512,512]{2,1,0:T(8,128)}) %all-gather.5.cloned.1.call-update) | async-done | bytes 1048592 | tf_op jit(solution)/shard_map/all_gather | solution.py:29
  39.6 2.2 bitcast_convert_fusion
  41.8 2.1 collective-permute-start.1
  46.0 2.9 collective-permute-done
  49.0 2.5 pad_maximum_fusion
  51.5 3.4 gather_fusion
  54.9 5.5 %fusion.30 = f32[512,512]{1,0:T(8,128)} fusion(bf16[4,1,512,512]{3,2,1,0:T(8,128)(2,1)S(1)} %copy-done, bf16[4,512,512]{2,1,0:T(8,128)(2,1)} %gather_fusion, bf16[4,1,512,512]{3,2,1,0:T(8,128)(2,1)} %param.6), kind=kOutput, calls=%fused_computation.24 | convolution fusion | flops 2148532224 | bytes 7340032 | tf_op jit(solution)/shard_map/tij,tkj->tik/dot_general | solution.py:21
  61.3 59.4 %all-reduce.7.cloned.1.call-done = f32[512,512]{1,0:T(8,128)} async-done(((f32[512,512]{1,0:T(8,128)}), f32[512,512]{1,0:T(8,128)}) %all-reduce.7.cloned.1.call-update) | async-done | bytes 1048592 | tf_op jit(solution)/shard_map/psum | solution.py:37
  120.6 2.2 fusion.55
  122.8 14.7 %all-reduce.2 = (f32[]{:T(128)}, f32[]{:T(128)}) all-reduce(f32[]{:T(128)} %get-tuple-element.10, f32[]{:T(128)} %get-tuple-element.9), channel_id=1, replica_groups=mesh['sector'=8,'term'=4] {'sector'}, use_global_device_ids=true, to_apply=%region_2.0 | all-reduce | flops 2 | bytes 16 | tf_op jit(solution)/shard_map/psum | solution.py:38
  138.8 10.7 %all-gather.7.cloned.1.call-done = f32[1,512,512]{2,1,0:T(8,128)} async-done(((f32[1,128,512]{2,1,0:T(8,128)}), f32[1,512,512]{2,1,0:T(8,128)}) %all-gather.7.cloned.1.call-update) | async-done | bytes 1048592 | tf_op jit(solution)/shard_map/all_gather | solution.py:30
  149.5 2.8 multiply_reduce_fusion.6
  152.4 13.7 %psum.87 = f32[]{:T(128)} all-reduce(f32[]{:T(128)} %get-tuple-element.21), channel_id=1, replica_groups=mesh['sector'=8,'term'=4] {'sector'}, use_global_device_ids=true, to_apply=%region_6.0 | all-reduce | flops 1 | bytes 8 | tf_op jit(solution)/shard_map/psum | solution.py:41
  169.7 2.3 collective-permute-done.2
  173.4 3.4 gather_fusion.1
  176.8 5.5 %fusion.37 = f32[512,512]{1,0:T(8,128)} fusion(bf16[4,1,512,512]{3,2,1,0:T(8,128)(2,1)S(1)} %copy-done, bf16[4,512,512]{2,1,0:T(8,128)(2,1)} %gather_fusion.1, bf16[4,1,512,512]{3,2,1,0:T(8,128)(2,1)} %param.6), kind=kOutput, calls=%fused_computation.25 | convolution fusion | flops 2148532224 | bytes 7340032 | tf_op jit(solution)/shard_map/tij,tkj->tik/dot_general | solution.py:21
  182.4 60.9 %all-reduce.9.cloned.1.call-done = f32[512,512]{1,0:T(8,128)} async-done(((f32[512,512]{1,0:T(8,128)}), f32[512,512]{1,0:T(8,128)}) %all-reduce.9.cloned.1.call-update) | async-done | bytes 1048592 | tf_op jit(solution)/shard_map/psum | solution.py:37
  243.3 2.2 multiply_reduce_fusion.4
  245.5 14.3 %all-reduce.1 = (f32[]{:T(128)}, f32[]{:T(128)}) all-reduce(f32[]{:T(128)} %get-tuple-element.8, f32[]{:T(128)} %get-tuple-element.7), channel_id=1, replica_groups=mesh['sector'=8,'term'=4] {'sector'}, use_global_device_ids=true, to_apply=%region_9.0 | all-reduce | flops 2 | bytes 16 | tf_op jit(solution)/shard_map/psum | solution.py:38
  261.1 3.6 multiply_reduce_fusion.3
  264.6 12.4 %psum.91 = f32[]{:T(128)} all-reduce(f32[]{:T(128)} %get-tuple-element.19), channel_id=1, replica_groups=mesh['sector'=8,'term'=4] {'sector'}, use_global_device_ids=true, to_apply=%region_13.0 | all-reduce | flops 1 | bytes 8 | tf_op jit(solution)/shard_map/psum | solution.py:41
  277.8 1.3 fusion.59
  279.1 1.8 collective-permute-start.5
  282.4 2.3 collective-permute-done.4
  286.0 3.4 gather_fusion.2
  289.5 5.5 %fusion.44 = f32[512,512]{1,0:T(8,128)} fusion(bf16[4,1,512,512]{3,2,1,0:T(8,128)(2,1)S(1)} %copy-done, bf16[4,512,512]{2,1,0:T(8,128)(2,1)} %gather_fusion.2, bf16[4,1,512,512]{3,2,1,0:T(8,128)(2,1)} %param.6), kind=kOutput, calls=%fused_computation.26 | convolution fusion | flops 2148532224 | bytes 7340032 | tf_op jit(solution)/shard_map/tij,tkj->tik/dot_general | solution.py:21
  295.0 59.5 %all-reduce.11.cloned.1.call-done = f32[512,512]{1,0:T(8,128)} async-done(((f32[512,512]{1,0:T(8,128)}), f32[512,512]{1,0:T(8,128)}) %all-reduce.11.cloned.1.call-update) | async-done | bytes 1048592 | tf_op jit(solution)/shard_map/psum | solution.py:37
  354.5 2.2 multiply_reduce_fusion.1
  356.7 14.3 %all-reduce = (f32[]{:T(128)}, f32[]{:T(128)}) all-reduce(f32[]{:T(128)} %get-tuple-element.6, f32[]{:T(128)} %get-tuple-element.5), channel_id=1, replica_groups=mesh['sector'=8,'term'=4] {'sector'}, use_global_device_ids=true, to_apply=%region_16.0 | all-reduce | flops 2 | bytes 16 | tf_op jit(solution)/shard_map/psum | solution.py:38
  372.3 3.6 multiply_reduce_fusion
  375.8 12.4 %psum.95 = f32[]{:T(128)} all-reduce(f32[]{:T(128)} %get-tuple-element.17), channel_id=1, replica_groups=mesh['sector'=8,'term'=4] {'sector'}, use_global_device_ids=true, to_apply=%region_20.0 | all-reduce | flops 1 | bytes 8 | tf_op jit(solution)/shard_map/psum | solution.py:41
  388.9 1.7 fusion.57
  (31 shorter events, 10.7 us)
Async XLA Ops:
  6.5 48.4 %copy-start = (bf16[4,1,512,512]{3,2,1,0:T(8,128)(2,1)S(1)}, bf16[4,1,512,512]{3,2,1,0:T(8,128)(2,1)}, u32[]{:S(2)}) copy-start(bf16[4,1,512,512]{3,2,1,0:T(8,128)(2,1)} %param.7) | copy-start | bytes 6291460
  6.5 33.1 %all-gather.5.cloned.1.call-start = ((), (), s32[]{:S(2)}) async-start(), calls=%async_computation.3 | async-start | bytes 1310720 | tf_op jit(solution)/shard_map/all_gather | solution.py:29
  7.3 113.4 %all-reduce.7.cloned.1.call-start = ((), (), s32[]{:S(2)}) async-start(), calls=%async_computation | async-start | bytes 2097152 | tf_op jit(solution)/shard_map/psum | solution.py:37
  39.6 6.3 %copy-start.2 = (f32[1,512,512]{2,1,0:T(8,128)S(1)}, f32[1,512,512]{2,1,0:T(8,128)}, u32[]{:S(2)}) copy-start(f32[1,512,512]{2,1,0:T(8,128)} %all-gather.5.cloned.1.call-done) | copy-start | bytes 3145732
  41.8 4.2 %collective-permute-start.1 = (bf16[512,512]{1,0:T(8,128)(2,1)}, bf16[512,512]{1,0:T(8,128)(2,1)}, u32[]{:S(2)}, u32[]{:S(2)}) collective-permute-start(bf16[512,512]{1,0:T(8,128)(2,1)} %bitcast_convert_fusion), channel_id=1, source_target_pairs={{0,4},{4,8},{8,12},{12,16},{16,20},{20,24},{24,28},{1,5},{5,9},{9,... | collective-permute-start | bytes 1572872 | tf_op jit(solution)/shard_map/ppermute | solution.py:12
  43.9 5.0 %collective-permute-start = (bf16[512,512]{1,0:T(8,128)(2,1)}, bf16[512,512]{1,0:T(8,128)(2,1)}, u32[]{:S(2)}, u32[]{:S(2)}) collective-permute-start(bf16[512,512]{1,0:T(8,128)(2,1)} %bitcast_convert_fusion), channel_id=1, source_target_pairs={{4,0},{8,4},{12,8},{16,12},{20,16},{24,20},{28,24},{5,1},{9,5},{13... | collective-permute-start | bytes 1572872 | tf_op jit(solution)/shard_map/ppermute | solution.py:12
  60.5 89.0 %all-gather.7.cloned.1.call-start = ((), (), s32[]{:S(2)}) async-start(), calls=%async_computation.4 | async-start | bytes 1310720 | tf_op jit(solution)/shard_map/all_gather | solution.py:30
  61.2 182.1 %all-reduce.9.cloned.1.call-start = ((), (), s32[]{:S(2)}) async-start(), calls=%async_computation.1 | async-start | bytes 2097152 | tf_op jit(solution)/shard_map/psum | solution.py:37
  166.9 2.8 collective-permute-start.3
  168.2 3.8 collective-permute-start.2
  182.4 172.1 %all-reduce.11.cloned.1.call-start = ((), (), s32[]{:S(2)}) async-start(), calls=%async_computation.2 | async-start | bytes 2097152 | tf_op jit(solution)/shard_map/psum | solution.py:37
  264.6 17.6 %copy-start.1 = (f32[512,512]{1,0:T(8,128)S(1)}, f32[512,512]{1,0:T(8,128)}, u32[]{:S(2)}) copy-start(f32[512,512]{1,0:T(8,128)} %get-tuple-element.20) | copy-start | bytes 3145732
  279.1 3.3 collective-permute-start.5
  280.9 3.8 collective-permute-start.4
Sparse Core Ops, SparseCore 0:
  8.9 30.6 all-gather.4
  60.6 59.9 all-reduce.6
  122.2 27.2 all-gather.6
  182.5 60.7 all-reduce.8
  295.2 59.3 all-reduce.10
where the time goes:
time: 398 us; the launch traced here: 397 us
  waiting for transfers between devices  232 us (58%)
  blocking collectives  81.9 us (21%)
  other arithmetic  28 us (7%)
  between operations  19.1 us (5%)
  matrix products  16.6 us (4%)
  local copies, waits for them, and re-layouts  10.3 us (3%)
  starting transfers between devices  9.25 us (2%)
    psum x3, waiting for transfers between devices, per_device(): hpsi = lax.psum(partial_image, 'term')  180 us
    psum x3, blocking collectives, per_device(): lax.psum((jnp.sum(psi * hpsi), jnp.sum(psi * psi)), 'sector')  43.4 us
    psum x3, blocking collectives, per_device(): total = lax.psum(jnp.sum(fresh * fresh), 'sector')  38.6 us
    all_gather x1, waiting for transfers between devices, per_device(): lax.all_gather(wave[0], 'term', axis=0, tiled=True)  32.3 us
    dot_general x3, matrix products, apply_terms(): jnp.einsum('tij,tkj->tik', inner, right_ops[:, 0], preferred_element_type...  16.6 us
    all_gather x1, waiting for transfers between devices, per_device(): lax.all_gather(diag[0], 'term', axis=0, tiled=True)  10.7 us
    gather x3, local copies, waits for them, and re-layouts, apply_terms(): picked = stacked[my_charges + 1]  10.3 us
    reduce_sum x3, other arithmetic, per_device(): total = lax.psum(jnp.sum(fresh * fresh), 'sector')  9.95 us
  transfers between devices with their start and end apart: 11, of which 10 were waited for; matrix products, arithmetic and copies ran while one was open for 1% of the time, Pallas kernels for 0%

commit v1 on v0

--- a/solution.py
+++ b/solution.py
@@ -34,7 +34,7 @@
         lower = from_behind(wb, "sector", 1)
         upper = from_behind(wb, "sector", -1)
         partial_image = apply_terms(left_ops, right_ops, my_charges, wb, lower, upper)
-        hpsi = lax.psum(partial_image, "term")
+        hpsi = jnp.sum(lax.all_gather(partial_image, "term"), axis=0)
         cross, square = lax.psum((jnp.sum(psi * hpsi), jnp.sum(psi * psi)), "sector")
         theta = cross / square
         fresh = psi - (hpsi - theta * psi) / jnp.maximum(jnp.abs(full_diag - theta), 1.0)

time: 398 us -> 490 us (1.23)
  waiting for transfers between devices: 232 us -> 313 us
  other arithmetic: 28 us -> 39.4 us
    all_gather x0 -> x3, waiting for transfers between devices: none -> 266 us  [per_device(): hpsi = jnp.sum(lax.all_gather(partial_image, 'term'), axis=0)]
    psum x3 -> x0, waiting for transfers between devices: 180 us -> none  [per_device(): hpsi = lax.psum(partial_image, 'term')]
    reduce_sum x0 -> x3, other arithmetic: none -> 11.4 us  [per_device(): hpsi = jnp.sum(lax.all_gather(partial_image, 'term'), axis=0)]
where the time goes in v1:
time: 490 us
  waiting for transfers between devices  313 us (64%)
  blocking collectives  81.3 us (17%)
  other arithmetic  39.4 us (8%)
  between operations  19.1 us (4%)
  matrix products  16.7 us (3%)
  local copies, waits for them, and re-layouts  10.3 us (2%)
  starting transfers between devices  9.25 us (2%)
    all_gather x3, waiting for transfers between devices, per_device(): hpsi = jnp.sum(lax.all_gather(partial_image, 'term'), axis=0)  266 us
    psum x3, blocking collectives, per_device(): lax.psum((jnp.sum(psi * hpsi), jnp.sum(psi * psi)), 'sector')  42.7 us
    psum x3, blocking collectives, per_device(): total = lax.psum(jnp.sum(fresh * fresh), 'sector')  38.6 us
    all_gather x1, waiting for transfers between devices, per_device(): lax.all_gather(wave[0], 'term', axis=0, tiled=True)  32.3 us
    dot_general x3, matrix products, apply_terms(): jnp.einsum('tij,tkj->tik', inner, right_ops[:, 0], preferred_element_type...  16.7 us
    reduce_sum x3, other arithmetic, per_device(): hpsi = jnp.sum(lax.all_gather(partial_image, 'term'), axis=0)  11.4 us
    gather x3, local copies, waits for them, and re-layouts, apply_terms(): picked = stacked[my_charges + 1]  10.3 us
    reduce_sum x3, other arithmetic, per_device(): total = lax.psum(jnp.sum(fresh * fresh), 'sector')  9.92 us
  transfers between devices with their start and end apart: 11, of which 10 were waited for; matrix products, arithmetic and copies ran while one was open for 1% of the time, Pallas kernels for 0%

profile of v1, /device:TPU:0, one launch (start us, length us, event | category | flops | bytes accessed | tf_op | source)
XLA Modules:
  0.0 489.5 jit_solution(11015255673384898556)
XLA Ops:
  7.3 32.3 %all-gather.11.cloned.1.call-done = f32[1,512,512]{2,1,0:T(8,128)} async-done(((f32[1,128,512]{2,1,0:T(8,128)}), f32[1,512,512]{2,1,0:T(8,128)}) %all-gather.11.cloned.1.call-update) | async-done | bytes 1048592 | tf_op jit(solution)/shard_map/all_gather | solution.py:29
  39.6 2.2 bitcast_convert_fusion
  41.8 2.1 collective-permute-start.1
  46.1 2.9 collective-permute-done
  49.0 2.5 pad_maximum_fusion
  51.5 3.4 gather_fusion
  54.9 5.6 %fusion.30 = f32[512,512]{1,0:T(8,128)} fusion(bf16[4,1,512,512]{3,2,1,0:T(8,128)(2,1)S(1)} %copy-done, bf16[4,512,512]{2,1,0:T(8,128)(2,1)} %gather_fusion, bf16[4,1,512,512]{3,2,1,0:T(8,128)(2,1)} %param.6), kind=kOutput, calls=%fused_computation.24 | convolution fusion | flops 2148532224 | bytes 7340032 | tf_op jit(solution)/shard_map/tij,tkj->tik/dot_general | solution.py:21
  61.3 88.2 %all-gather.13.cloned.1.call-done = f32[2048,512]{1,0:T(8,128)} async-done(((f32[512,512]{1,0:T(8,128)}), f32[2048,512]{1,0:T(8,128)}) %all-gather.13.cloned.1.call-update) | async-done | bytes 4194320 | tf_op jit(solution)/shard_map/all_gather | solution.py:37
  149.5 3.8 reduce_sum.120
  153.3 2.2 fusion.55
  155.5 14.5 %all-reduce.2 = (f32[]{:T(128)}, f32[]{:T(128)}) all-reduce(f32[]{:T(128)} %get-tuple-element.10, f32[]{:T(128)} %get-tuple-element.9), channel_id=1, replica_groups=mesh['sector'=8,'term'=4] {'sector'}, use_global_device_ids=true, to_apply=%region_2.0 | all-reduce | flops 2 | bytes 16 | tf_op jit(solution)/shard_map/psum | solution.py:38
  171.3 6.3 %all-gather.15.cloned.1.call-done = f32[1,512,512]{2,1,0:T(8,128)} async-done(((f32[1,128,512]{2,1,0:T(8,128)}), f32[1,512,512]{2,1,0:T(8,128)}) %all-gather.15.cloned.1.call-update) | async-done | bytes 1048592 | tf_op jit(solution)/shard_map/all_gather | solution.py:30
  177.6 2.8 multiply_reduce_fusion.6
  180.5 13.7 %psum.65 = f32[]{:T(128)} all-reduce(f32[]{:T(128)} %get-tuple-element.21), channel_id=1, replica_groups=mesh['sector'=8,'term'=4] {'sector'}, use_global_device_ids=true, to_apply=%region_6.0 | all-reduce | flops 1 | bytes 8 | tf_op jit(solution)/shard_map/psum | solution.py:41
  197.9 2.3 collective-permute-done.2
  201.5 3.4 gather_fusion.1
  204.9 5.6 %fusion.37 = f32[512,512]{1,0:T(8,128)} fusion(bf16[4,1,512,512]{3,2,1,0:T(8,128)(2,1)S(1)} %copy-done, bf16[4,512,512]{2,1,0:T(8,128)(2,1)} %gather_fusion.1, bf16[4,1,512,512]{3,2,1,0:T(8,128)(2,1)} %param.6), kind=kOutput, calls=%fused_computation.25 | convolution fusion | flops 2148532224 | bytes 7340032 | tf_op jit(solution)/shard_map/tij,tkj->tik/dot_general | solution.py:21
  210.6 89.8 %all-gather.17.cloned.1.call-done = f32[2048,512]{1,0:T(8,128)} async-done(((f32[512,512]{1,0:T(8,128)}), f32[2048,512]{1,0:T(8,128)}) %all-gather.17.cloned.1.call-update) | async-done | bytes 4194320 | tf_op jit(solution)/shard_map/all_gather | solution.py:37
  300.3 3.8 reduce_sum.124
  304.1 2.2 multiply_reduce_fusion.4
  306.3 14.1 %all-reduce.1 = (f32[]{:T(128)}, f32[]{:T(128)}) all-reduce(f32[]{:T(128)} %get-tuple-element.8, f32[]{:T(128)} %get-tuple-element.7), channel_id=1, replica_groups=mesh['sector'=8,'term'=4] {'sector'}, use_global_device_ids=true, to_apply=%region_9.0 | all-reduce | flops 2 | bytes 16 | tf_op jit(solution)/shard_map/psum | solution.py:38
  321.7 3.5 multiply_reduce_fusion.3
  325.2 12.4 %psum.68 = f32[]{:T(128)} all-reduce(f32[]{:T(128)} %get-tuple-element.19), channel_id=1, replica_groups=mesh['sector'=8,'term'=4] {'sector'}, use_global_device_ids=true, to_apply=%region_13.0 | all-reduce | flops 1 | bytes 8 | tf_op jit(solution)/shard_map/psum | solution.py:41
  342.9 2.3 collective-permute-done.4
  346.6 3.4 gather_fusion.2
  350.0 5.6 %fusion.44 = f32[512,512]{1,0:T(8,128)} fusion(bf16[4,1,512,512]{3,2,1,0:T(8,128)(2,1)S(1)} %copy-done, bf16[4,512,512]{2,1,0:T(8,128)(2,1)} %gather_fusion.2, bf16[4,1,512,512]{3,2,1,0:T(8,128)(2,1)} %param.6), kind=kOutput, calls=%fused_computation.26 | convolution fusion | flops 2148532224 | bytes 7340032 | tf_op jit(solution)/shard_map/tij,tkj->tik/dot_general | solution.py:21
  355.6 87.7 %all-gather.19.cloned.1.call-done = f32[2048,512]{1,0:T(8,128)} async-done(((f32[512,512]{1,0:T(8,128)}), f32[2048,512]{1,0:T(8,128)}) %all-gather.19.cloned.1.call-update) | async-done | bytes 4194320 | tf_op jit(solution)/shard_map/all_gather | solution.py:37
  443.3 3.8 reduce_sum.128
  447.1 2.2 multiply_reduce_fusion.1
  449.3 14.1 %all-reduce = (f32[]{:T(128)}, f32[]{:T(128)}) all-reduce(f32[]{:T(128)} %get-tuple-element.6, f32[]{:T(128)} %get-tuple-element.5), channel_id=1, replica_groups=mesh['sector'=8,'term'=4] {'sector'}, use_global_device_ids=true, to_apply=%region_16.0 | all-reduce | flops 2 | bytes 16 | tf_op jit(solution)/shard_map/psum | solution.py:38
  464.7 3.5 multiply_reduce_fusion
  468.2 12.4 %psum.71 = f32[]{:T(128)} all-reduce(f32[]{:T(128)} %get-tuple-element.17), channel_id=1, replica_groups=mesh['sector'=8,'term'=4] {'sector'}, use_global_device_ids=true, to_apply=%region_20.0 | all-reduce | flops 1 | bytes 8 | tf_op jit(solution)/shard_map/psum | solution.py:41
  (34 shorter events, 15.6 us)
Async XLA Ops:
  6.5 48.4 %copy-start = (bf16[4,1,512,512]{3,2,1,0:T(8,128)(2,1)S(1)}, bf16[4,1,512,512]{3,2,1,0:T(8,128)(2,1)}, u32[]{:S(2)}) copy-start(bf16[4,1,512,512]{3,2,1,0:T(8,128)(2,1)} %param.7) | copy-start | bytes 6291460
  6.5 33.1 %all-gather.11.cloned.1.call-start = ((), (), s32[]{:S(2)}) async-start(), calls=%async_computation | async-start | bytes 1310720 | tf_op jit(solution)/shard_map/all_gather | solution.py:29
  7.3 142.3 %all-gather.13.cloned.1.call-start = ((), (), s32[]{:S(2)}) async-start(), calls=%async_computation.1 | async-start | bytes 5242880 | tf_op jit(solution)/shard_map/all_gather | solution.py:37
  39.6 6.3 %copy-start.2 = (f32[1,512,512]{2,1,0:T(8,128)S(1)}, f32[1,512,512]{2,1,0:T(8,128)}, u32[]{:S(2)}) copy-start(f32[1,512,512]{2,1,0:T(8,128)} %all-gather.11.cloned.1.call-done) | copy-start | bytes 3145732
  41.8 4.2 collective-permute-start.1
  43.9 5.0 %collective-permute-start = (bf16[512,512]{1,0:T(8,128)(2,1)}, bf16[512,512]{1,0:T(8,128)(2,1)}, u32[]{:S(2)}, u32[]{:S(2)}) collective-permute-start(bf16[512,512]{1,0:T(8,128)(2,1)} %bitcast_convert_fusion), channel_id=1, source_target_pairs={{4,0},{8,4},{12,8},{16,12},{20,16},{24,20},{28,24},{5,1},{9,5},{13... | collective-permute-start | bytes 1572872 | tf_op jit(solution)/shard_map/ppermute | solution.py:12
  60.5 117.1 %all-gather.15.cloned.1.call-start = ((), (), s32[]{:S(2)}) async-start(), calls=%async_computation.2 | async-start | bytes 1310720 | tf_op jit(solution)/shard_map/all_gather | solution.py:30
  61.3 239.1 %all-gather.17.cloned.1.call-start = ((), (), s32[]{:S(2)}) async-start(), calls=%async_computation.3 | async-start | bytes 5242880 | tf_op jit(solution)/shard_map/all_gather | solution.py:37
  195.0 2.8 collective-permute-start.3
  196.4 3.8 collective-permute-start.2
  210.5 232.8 %all-gather.19.cloned.1.call-start = ((), (), s32[]{:S(2)}) async-start(), calls=%async_computation.4 | async-start | bytes 5242880 | tf_op jit(solution)/shard_map/all_gather | solution.py:37
  325.2 17.6 %copy-start.1 = (f32[512,512]{1,0:T(8,128)S(1)}, f32[512,512]{1,0:T(8,128)}, u32[]{:S(2)}) copy-start(f32[512,512]{1,0:T(8,128)} %get-tuple-element.20) | copy-start | bytes 3145732
  339.6 3.3 collective-permute-start.5
  341.5 3.8 collective-permute-start.4
Sparse Core Ops, SparseCore 0:
  8.9 30.6 all-gather.10
  60.6 88.8 all-gather.12
  151.1 26.4 all-gather.14
  210.7 89.6 all-gather.16
  355.7 87.5 all-gather.18
